TPU v7x, 32 devices: a whole 2x2x4 slice. The times are simulated.
32 devices in a mesh: batch: 4 (over y, x), ctx: 8 (over z, core).
Axes of the slice: x: 2, y: 2, z: 4, core: 2. Of those that a mesh axis runs over, the one named last changes fastest.
Arguments:
- hidden: bfloat16 [4, 1024, 768], P('batch', 'ctx'), may hold values from -6 to 6
- cotangent: bfloat16 [4, 1024, 768], P('batch', 'ctx'), may hold values from -6 to 6
- w_qkv: bfloat16 [768, 2304], P(('batch', 'ctx')), may hold values from -3 to 3
- w_proj: bfloat16 [768, 768], P(('batch', 'ctx')), may hold values from -1.25 to 1.25
- w_inner: bfloat16 [768, 2304], P(('batch', 'ctx')), may hold values from -0.21875 to 0.21875
- w_down: bfloat16 [768, 1152], P(('batch', 'ctx')), may hold values from -0.1875 to 0.1875
- norm1_gain: bfloat16 [768], P(('batch', 'ctx')), may hold values from 0.5 to 1.5
- norm2_gain: bfloat16 [768], P(('batch', 'ctx')), may hold values from 0.5 to 1.5
Outputs:
- hidden_out: bfloat16 [4, 1024, 768], P('batch', 'ctx')
- hidden_grad: float32 [4, 1024, 768], P('batch', 'ctx')
- qkv_grad: float32 [768, 2304], P(('batch', 'ctx'))
- proj_grad: float32 [768, 768], P(('batch', 'ctx'))
- inner_grad: float32 [768, 2304], P(('batch', 'ctx'))
- down_grad: float32 [768, 1152], P(('batch', 'ctx'))
- norm1_grad: float32 [768], P(('batch', 'ctx'))
- norm2_grad: float32 [768], P(('batch', 'ctx'))
All inputs are finite; a program needn't handle non-finite values.
Results may differ from a plain program's by a relative error of at most 0.02.
Values may be sent and summed in bfloat16 or wider, within the bound.
A program may use at most 192 MiB of HBM per device.

v0:
```python
import jax
import jax.numpy as jnp
from jax import lax
from jax.sharding import PartitionSpec as P

D = 768
HEADS = 12
HEAD_DIM = 64
FF = 1152
norm_eps = 1e-05
rope_base = 160000.0


def apply_layer_norm(values, gain_vector):
    centre = jnp.mean(values, axis=-1, keepdims=True)
    shifted = values - centre
    spread = jnp.mean(shifted * shifted, axis=-1, keepdims=True)
    inverse = lax.rsqrt(spread + norm_eps)
    normed = shifted * inverse
    return (normed * gain_vector, normed, inverse)


def layer_norm_gradient(upstream, gain_vector, normed, inverse):
    scaled = upstream * gain_vector
    first_mean = jnp.mean(scaled, axis=-1, keepdims=True)
    second_mean = jnp.mean(scaled * normed, axis=-1, keepdims=True)
    return (
        inverse * (scaled - first_mean - normed * second_mean),
        jnp.sum(upstream * normed, axis=0),
    )


def rope_tables(offset, row_count, head_width):
    half_dim = head_width // 2
    position = (offset + jnp.arange(row_count, dtype=jnp.int32)).astype(jnp.float32)
    exponent = jnp.arange(half_dim, dtype=jnp.int32).astype(jnp.float32) * (-2.0 / head_width)
    angles = position[:, None] * jnp.power(rope_base, exponent)[None, :]
    return (jnp.cos(angles), jnp.sin(angles))


def rotate(values, cosine, sine_table, direction):
    half_dim = values.shape[-1] // 2
    front_half = values[..., :half_dim]
    back_half = values[..., half_dim:]
    cos_rows = cosine[:, None, :]
    sin_rows = sine_table[:, None, :] * direction
    return jnp.concatenate(
        [
            front_half * cos_rows - back_half * sin_rows,
            back_half * cos_rows + front_half * sin_rows,
        ],
        axis=-1,
    )


def gelu_parts(act_input):
    normal_cdf = 0.5 * (1.0 + jax.scipy.special.erf(act_input * 0.7071067811865476))
    density = jnp.exp(-0.5 * act_input * act_input) * 0.3989422804014327
    return (act_input * normal_cdf, normal_cdf + act_input * density)


def as_heads(flat_rows):
    return flat_rows.reshape(flat_rows.shape[0], HEADS, HEAD_DIM)


def pair_terms(query_rows, grad_rows, log_rows, delta_rows, key_rows, value_rows, score_scale):
    scores = (
        jnp.einsum("qhd,khd->hqk", query_rows, key_rows, preferred_element_type=jnp.float32)
        * score_scale
    )
    probabilities = jnp.exp(scores - log_rows[..., None])
    grad_dots = jnp.einsum(
        "qhd,khd->hqk", grad_rows, value_rows, preferred_element_type=jnp.float32
    )
    dscore = (probabilities * (grad_dots - delta_rows[..., None])).astype(jnp.bfloat16)
    return (probabilities.astype(jnp.bfloat16), dscore)


def local(hidden, cotangent, w_qkv, w_proj, w_inner, w_down, norm1_gain, norm2_gain):
    token_rows = hidden.shape[1]
    score_scale = HEAD_DIM ** (-0.5)
    full_qkv, full_proj, full_inner, full_down, gain_first, gain_second = (
        lax.all_gather(w_qkv, ("batch", "ctx"), axis=0, tiled=True),
        lax.all_gather(w_proj, ("batch", "ctx"), axis=0, tiled=True),
        lax.all_gather(w_inner, ("batch", "ctx"), axis=0, tiled=True),
        lax.all_gather(w_down, ("batch", "ctx"), axis=0, tiled=True),
        lax.all_gather(norm1_gain, ("batch", "ctx"), axis=0, tiled=True),
        lax.all_gather(norm2_gain, ("batch", "ctx"), axis=0, tiled=True),
    )
    first_norm_gain = gain_first.astype(jnp.float32)
    second_norm_gain = gain_second.astype(jnp.float32)
    input_tokens = hidden[0].astype(jnp.float32)
    first_normed_rows, first_centered_rows, first_inverse_deviation = apply_layer_norm(
        input_tokens, first_norm_gain
    )
    h_one = first_normed_rows.astype(jnp.bfloat16)
    projected = jnp.dot(h_one, full_qkv, preferred_element_type=jnp.float32)
    cosine, sine_table = rope_tables(lax.axis_index("ctx") * token_rows, token_rows, HEAD_DIM)
    query_rot = rotate(as_heads(projected[:, :D]), cosine, sine_table, 1.0).astype(jnp.bfloat16)
    key_flat = (
        rotate(as_heads(projected[:, D : 2 * D]), cosine, sine_table, 1.0)
        .astype(jnp.bfloat16)
        .reshape(token_rows, D)
    )
    value_flat = projected[:, 2 * D :].astype(jnp.bfloat16)
    key_rot = as_heads(key_flat)
    value_rows = as_heads(value_flat)
    zero_heads = jnp.zeros((token_rows, HEADS, HEAD_DIM), jnp.float32)
    piece_rows = (
        lax.all_gather(key_flat, "ctx", axis=0, tiled=True),
        lax.all_gather(value_flat, "ctx", axis=0, tiled=True),
    )
    row_peak = jnp.full((HEADS, token_rows), -jnp.inf, jnp.float32)
    row_total = jnp.zeros((HEADS, token_rows), jnp.float32)
    key_piece = as_heads(piece_rows[0])
    value_piece = as_heads(piece_rows[1])
    scores = (
        jnp.einsum("qhd,khd->hqk", query_rot, key_piece, preferred_element_type=jnp.float32)
        * score_scale
    )
    new_peak = jnp.max(scores, axis=-1)
    row_fade = jnp.exp(row_peak - new_peak)
    probabilities = jnp.exp(scores - new_peak[..., None])
    new_total = row_total * row_fade + jnp.sum(probabilities, axis=-1)
    new_mixture = zero_heads * jnp.transpose(row_fade)[:, :, None] + jnp.einsum(
        "hqk,khd->qhd",
        probabilities.astype(jnp.bfloat16),
        value_piece,
        preferred_element_type=jnp.float32,
    )
    log_total = new_peak + jnp.log(new_total)
    attended = (
        (new_mixture / jnp.transpose(new_total)[:, :, None])
        .reshape(token_rows, D)
        .astype(jnp.bfloat16)
    )
    residual_stream = input_tokens + jnp.dot(
        attended, full_proj, preferred_element_type=jnp.float32
    )
    second_normed_rows, second_centered_rows, second_inverse_deviation = apply_layer_norm(
        residual_stream, second_norm_gain
    )
    h_two = second_normed_rows.astype(jnp.bfloat16)
    inner_all = jnp.dot(h_two, full_inner, preferred_element_type=jnp.float32)
    act_half = inner_all[:, :FF]
    gate_half = inner_all[:, FF:]
    activated, gelu_slope = gelu_parts(act_half)
    middle = (activated * gate_half).astype(jnp.bfloat16)
    output_rows = residual_stream + jnp.einsum(
        "tf,df->td", middle, full_down, preferred_element_type=jnp.float32
    )
    back_qkv, back_proj, back_inner, back_down = (full_qkv, full_proj, full_inner, full_down)
    upstream = cotangent[0]
    d_middle = jnp.dot(upstream, back_down, preferred_element_type=jnp.float32)
    d_inner = jnp.concatenate(
        [d_middle * gate_half * gelu_slope, d_middle * activated], axis=-1
    ).astype(jnp.bfloat16)
    second_hidden_gradient = jnp.einsum(
        "te,de->td", d_inner, back_inner, preferred_element_type=jnp.float32
    )
    residual_norm_gradient, second_gain_portion = layer_norm_gradient(
        second_hidden_gradient, second_norm_gain, second_centered_rows, second_inverse_deviation
    )
    d_resid = upstream.astype(jnp.float32) + residual_norm_gradient
    d_resid_low = d_resid.astype(jnp.bfloat16)
    d_attended = jnp.einsum(
        "td,ed->te", d_resid_low, back_proj, preferred_element_type=jnp.float32
    ).astype(jnp.bfloat16)
    grad_heads = as_heads(d_attended)
    row_delta = jnp.transpose(
        jnp.sum(grad_heads.astype(jnp.float32) * as_heads(attended).astype(jnp.float32), axis=-1)
    )
    log_whole, delta_whole = (
        lax.all_gather(log_total, "ctx", axis=1, tiled=True),
        lax.all_gather(row_delta, "ctx", axis=1, tiled=True),
    )
    piece_rows = (
        lax.all_gather(key_flat, "ctx", axis=0, tiled=True),
        lax.all_gather(value_flat, "ctx", axis=0, tiled=True),
    )
    key_part = as_heads(piece_rows[0])
    value_part = as_heads(piece_rows[1])
    probs_low, dscore = pair_terms(
        query_rot, grad_heads, log_total, row_delta, key_part, value_part, score_scale
    )
    query_grad = (
        jnp.einsum("hqk,khd->qhd", dscore, key_part, preferred_element_type=jnp.float32)
        * score_scale
    )
    piece_rows = (
        lax.all_gather(query_rot.reshape(token_rows, D), "ctx", axis=0, tiled=True),
        lax.all_gather(d_attended, "ctx", axis=0, tiled=True),
    )
    query_part = as_heads(piece_rows[0])
    grad_part = as_heads(piece_rows[1])
    probs_low, dscore = pair_terms(
        query_part, grad_part, log_whole, delta_whole, key_rot, value_rows, score_scale
    )
    key_sum = (
        jnp.einsum("hqk,qhd->khd", dscore, query_part, preferred_element_type=jnp.float32)
        * score_scale
    )
    value_sum = jnp.einsum("hqk,qhd->khd", probs_low, grad_part, preferred_element_type=jnp.float32)
    d_query = rotate(query_grad, cosine, sine_table, -1.0)
    d_key = rotate(key_sum, cosine, sine_table, -1.0)
    d_projected = jnp.concatenate(
        [
            d_query.reshape(token_rows, D),
            d_key.reshape(token_rows, D),
            value_sum.reshape(token_rows, D),
        ],
        axis=-1,
    ).astype(jnp.bfloat16)
    first_hidden_gradient = jnp.einsum(
        "te,de->td", d_projected, back_qkv, preferred_element_type=jnp.float32
    )
    input_norm_gradient, first_gain_portion = layer_norm_gradient(
        first_hidden_gradient, first_norm_gain, first_centered_rows, first_inverse_deviation
    )
    input_grad = d_resid + input_norm_gradient

    def grad_rows(start, count):
        return jnp.concatenate(
            [
                jnp.einsum("td,te->de", h_one, d_projected, preferred_element_type=jnp.float32),
                jnp.einsum("te,td->ed", attended, d_resid_low, preferred_element_type=jnp.float32),
                jnp.einsum("td,te->de", h_two, d_inner, preferred_element_type=jnp.float32),
                jnp.einsum("td,tf->df", upstream, middle, preferred_element_type=jnp.float32),
                first_gain_portion[:, None],
                second_gain_portion[:, None],
            ],
            axis=1,
        )

    owned_rows = D // lax.axis_size(("batch", "ctx"))
    grad_share = lax.psum_scatter(
        grad_rows(jnp.int32(0), owned_rows * lax.axis_size(("batch", "ctx"))),
        ("batch", "ctx"),
        scatter_dimension=0,
        tiled=True,
    )
    qkv_share = grad_share[:, : 3 * D]
    proj_share = grad_share[:, 3 * D : 4 * D]
    inner_share = grad_share[:, 4 * D : 4 * D + 2 * FF]
    down_share = grad_share[:, 4 * D + 2 * FF : 4 * D + 3 * FF]
    first_share = grad_share[:, 4 * D + 3 * FF]
    second_share = grad_share[:, 4 * D + 3 * FF + 1]
    return (
        output_rows.astype(jnp.bfloat16)[None],
        input_grad[None],
        qkv_share,
        proj_share,
        inner_share,
        down_share,
        first_share,
        second_share,
    )


def solution(mesh):
    placed = (
        P("batch", "ctx", None),
        P("batch", "ctx", None),
        P(("batch", "ctx"), None),
        P(("batch", "ctx"), None),
        P(("batch", "ctx"), None),
        P(("batch", "ctx"), None),
        P(("batch", "ctx")),
        P(("batch", "ctx")),
    )
    return jax.shard_map(
        local,
        mesh=mesh,
        in_specs=placed,
        out_specs=(
            P("batch", "ctx", None),
            P("batch", "ctx", None),
            P(("batch", "ctx"), None),
            P(("batch", "ctx"), None),
            P(("batch", "ctx"), None),
            P(("batch", "ctx"), None),
            P(("batch", "ctx")),
            P(("batch", "ctx")),
        ),
        check_vma=False,
    )
```

profile of v0, /device:TPU:0, one launch (start us, length us, event | category | flops | bytes accessed | tf_op | source)
XLA Modules:
  0.0 641.2 jit_solution(14519602445404281982)
XLA Ops:
  9.6 42.2 %all-reduce.2 = (bf16[768]{0:T(1024)(128)(2,1)S(1)}, bf16[768]{0:T(1024)(128)(2,1)S(1)}) all-reduce(bf16[768]{0:T(1024)(128)(2,1)S(1)} %dynamic-update-slice, bf16[768]{0:T(1024)(128)(2,1)S(1)} %dynamic-update-slice.1), channel_id=1, replica_groups=mesh['batch'=4,'ctx'=8] {'batch','ctx'}, use_global_device_ids=true, to_apply=%add | all-reduce | flops 1536 | bytes 6144
  54.8 19.1 %all-gather.9.cloned.1.call-done = bf16[768,2304]{1,0:T(8,128)(2,1)} async-done(((bf16[24,2304]{1,0:T(8,128)(2,1)}), bf16[768,2304]{1,0:T(8,128)(2,1)}) %all-gather.9.cloned.1.call-update) | async-done | bytes 3538960 | tf_op jit(solution)/shard_map/all_gather | solution.py:83
  73.9 2.8 fusion.79
  82.0 22.7 %all-gather.11.cloned.1.call-done = bf16[1024,768]{0,1:T(8,128)(2,1)} async-done(((bf16[128,768]{0,1:T(8,128)(2,1)}), bf16[1024,768]{0,1:T(8,128)(2,1)}) %all-gather.11.cloned.1.call-update) | async-done | bytes 1572880 | tf_op jit(solution)/shard_map/all_gather | solution.py:110
  109.9 21.1 %all-gather.13.cloned.1.call-done = bf16[1024,768]{1,0:T(8,128)(2,1)} async-done(((bf16[128,768]{1,0:T(8,128)(2,1)}), bf16[1024,768]{1,0:T(8,128)(2,1)}) %all-gather.13.cloned.1.call-update) | async-done | bytes 1572880 | tf_op jit(solution)/shard_map/all_gather | solution.py:111
  132.7 4.8 fusion.35
  137.5 49.6 %all-gather.15.cloned.1.call-done = bf16[768,768]{1,0:T(8,128)(2,1)} async-done(((bf16[24,768]{1,0:T(8,128)(2,1)}), bf16[768,768]{1,0:T(8,128)(2,1)}) %all-gather.15.cloned.1.call-update) | async-done | bytes 1179664 | tf_op jit(solution)/shard_map/all_gather | solution.py:84
  189.1 59.9 %all-gather.17.cloned.1.call-done = bf16[768,2304]{1,0:T(8,128)(2,1)} async-done(((bf16[24,2304]{1,0:T(8,128)(2,1)}), bf16[768,2304]{1,0:T(8,128)(2,1)}) %all-gather.17.cloned.1.call-update) | async-done | bytes 3538960 | tf_op jit(solution)/shard_map/all_gather | solution.py:85
  249.0 2.7 fusion.81
  251.6 54.4 %all-gather.19.cloned.1.call-done = bf16[768,1152]{1,0:T(8,128)(2,1)} async-done(((bf16[24,1152]{1,0:T(8,128)(2,1)}), bf16[768,1152]{1,0:T(8,128)(2,1)}) %all-gather.19.cloned.1.call-update) | async-done | bytes 1769488 | tf_op jit(solution)/shard_map/all_gather | solution.py:86
  314.4 15.1 %all_gather.47 = f32[12,1024]{1,0:T(8,128)} all-gather(f32[12,128]{1,0:T(8,128)S(1)} %get-tuple-element.36), channel_id=1, replica_groups=mesh['batch'=4,'ctx'=8] {'ctx'}, dimensions={1}, use_global_device_ids=true | all-gather | bytes 55296 | tf_op jit(solution)/shard_map/all_gather | solution.py:174
  329.6 15.2 %all_gather.49 = f32[12,1024]{1,0:T(8,128)} all-gather(f32[12,128]{1,0:T(8,128)S(1)} %bitcast.128), channel_id=1, replica_groups=mesh['batch'=4,'ctx'=8] {'ctx'}, dimensions={1}, use_global_device_ids=true | all-gather | bytes 55296 | tf_op jit(solution)/shard_map/all_gather | solution.py:175
  345.3 3.8 convolution_bitcast_fusion
  349.1 4.1 fusion.59
  353.2 5.1 fusion.85
  358.4 7.3 %fusion.23 = f32[128,12,64]{0,2,1:T(8,128)} fusion(bf16[1024,12,64]{0,2,1:T(8,128)(2,1)} %bitcast.114, f32[12,128,1024]{2,1,0:T(8,128)} %copy-done, f32[12,128]{1,0:T(8,128)S(1)} %bitcast.129, f32[12,128]{1,0:T(8,128)} %copy-done.21, bf16[128,12,64]{0,2,1:T(8,128)(2,1)} %bitcast.120, bf16[1024,12,64]{0,2,1:T(8,128)(2,1)} %bitcast.110), kind=kOutput, calls=%fused_computation.25 | convolution fusion | flops 410615808 | bytes 10039296 | tf_op jit(solution)/shard_map/hqk,khd->qhd/dot_general | solution.py:187
  365.6 2.6 copy.29
  368.2 4.5 fusion.28
  372.7 8.9 %fusion.21 = f32[128,12,64]{0,2,1:T(8,128)} fusion(bf16[1024,12,64]{0,2,1:T(8,128)(2,1)} %bitcast.116, f32[12,1024,128]{2,1,0:T(8,128)} %fusion.85, f32[12,1024]{1,0:T(8,128)} %all_gather.49, f32[12,1024]{1,0:T(8,128)} %all_gather.47, bf16[1024,12,64]{0,2,1:T(8,128)(2,1)} %bitcast.106, bf16[128,12,64]{0,2,1:T(8,128)(2,1)} %bitcast.127), kind=kOutput, calls=%fused_computation.23 | convolution fusion | flops 410615808 | bytes 10125312 | tf_op jit(solution)/shard_map/hqk,qhd->khd/dot_general | solution.py:200
  383.0 4.1 fusion.61
  387.1 2.6 fusion.57
  390.6 22.2 %concatenate.31 = f32[768,6530]{1,0:T(8,128)} concatenate(f32[768,2304]{1,0:T(8,128)} %fusion.61, f32[768,768]{1,0:T(8,128)S(1)} %fusion.66, f32[768,2304]{1,0:T(8,128)} %fusion.59, f32[768,1152]{1,0:T(8,128)} %convolution_bitcast_fusion, f32[768,1]{1,0:T(8,128)} %broadcast_in_dim.18, f32[768,1]{1,0:T(8,128)} %broadcast_in_dim.19), dimensions={1} | concatenate | bytes 40120320 | tf_op jit(solution)/shard_map/concatenate | solution.py:223
  414.1 2.9 fusion.31
  417.9 210.3 %reduce-scatter.2.cloned.1.call-done = f32[24,6530]{1,0:T(8,128)} async-done(((f32[768,6530]{1,0:T(8,128)}), f32[24,6530]{1,0:T(8,128)}) %reduce-scatter.2.cloned.1.call-update) | async-done | bytes 626896 | tf_op jit(solution)/shard_map/reduce_scatter | solution.py:236
  (132 shorter events, 39.0 us)
Async XLA Ops:
  7.2 66.8 %all-gather.9.cloned.1.call-start = ((), (), s32[]{:S(2)}) async-start(), calls=%async_computation.1 | async-start | bytes 3649536 | tf_op jit(solution)/shard_map/all_gather | solution.py:83
  7.9 96.8 %all-gather.11.cloned.1.call-start = ((), (), s32[]{:S(2)}) async-start(), calls=%async_computation.2 | async-start | bytes 1769472 | tf_op jit(solution)/shard_map/all_gather | solution.py:110
  52.9 23.9 %copy-start.22 = (f32[128]{0:T(128)}, f32[128]{0:T(128)S(1)}, u32[]{:S(2)}) copy-start(f32[128]{0:T(128)S(1)} %broadcast_multiply_fusion.6) | copy-start | bytes 1540
  54.1 22.7 %copy-start.26 = (f32[128]{0:T(128)}, f32[128]{0:T(128)S(1)}, u32[]{:S(2)}) copy-start(f32[128]{0:T(128)S(1)} %add_rsqrt_fusion.1) | copy-start | bytes 1540
  54.8 22.3 %copy-start.20 = (f32[128,32]{0,1:T(8,128)}, f32[128,32]{0,1:T(8,128)S(1)}, u32[]{:S(2)}) copy-start(f32[128,32]{0,1:T(8,128)S(1)} %get-tuple-element.40) | copy-start | bytes 49156
  78.6 52.3 %all-gather.13.cloned.1.call-start = ((), (), s32[]{:S(2)}) async-start(), calls=%async_computation.3 | async-start | bytes 1769472 | tf_op jit(solution)/shard_map/all_gather | solution.py:111
  79.4 107.7 %all-gather.15.cloned.1.call-start = ((), (), s32[]{:S(2)}) async-start(), calls=%async_computation.4 | async-start | bytes 1216512 | tf_op jit(solution)/shard_map/all_gather | solution.py:84
  80.0 169.0 %all-gather.17.cloned.1.call-start = ((), (), s32[]{:S(2)}) async-start(), calls=%async_computation.5 | async-start | bytes 3649536 | tf_op jit(solution)/shard_map/all_gather | solution.py:85
  80.6 225.5 %all-gather.19.cloned.1.call-start = ((), (), s32[]{:S(2)}) async-start(), calls=%async_computation.6 | async-start | bytes 1824768 | tf_op jit(solution)/shard_map/all_gather | solution.py:86
  81.2 272.1 %all-gather.21.cloned.1.call-start = ((), (), s32[]{:S(2)}) async-start(), calls=%async_computation.7 | async-start | bytes 1769472 | tf_op jit(solution)/shard_map/all_gather | solution.py:191
  81.9 283.7 %all-gather.23.cloned.1.call-start = ((), (), s32[]{:S(2)}) async-start(), calls=%async_computation.8 | async-start | bytes 1769472 | tf_op jit(solution)/shard_map/all_gather | solution.py:192
  109.9 204.6 %copy-start.21 = (f32[12,128]{1,0:T(8,128)}, f32[12,128]{1,0:T(8,128)S(1)}, u32[]{:S(2)}) copy-start(f32[12,128]{1,0:T(8,128)S(1)} %get-tuple-element.36) | copy-start | bytes 18436
  132.7 4.8 copy-start.8
  132.7 54.4 %copy-start.1 = (bf16[1,128,768]{2,1,0:T(8,128)(2,1)S(1)}, bf16[1,128,768]{2,1,0:T(8,128)(2,1)}, u32[]{:S(2)}) copy-start(bf16[1,128,768]{2,1,0:T(8,128)(2,1)} %param.8) | copy-start | bytes 589828
  188.9 117.2 %copy-start.13 = (bf16[1,128,768]{2,1,0:T(8,128)(2,1)S(1)}, bf16[1,128,768]{2,1,0:T(8,128)(2,1)}, u32[]{:S(2)}) copy-start(bf16[1,128,768]{2,1,0:T(8,128)(2,1)} %param.9) | copy-start | bytes 589828
  188.9 121.2 %copy-start.24 = (f32[128]{0:T(128)}, f32[128]{0:T(128)S(1)}, u32[]{:S(2)}) copy-start(f32[128]{0:T(128)S(1)} %broadcast_multiply_fusion.5) | copy-start | bytes 1540
  189.1 121.0 %copy-start.28 = (f32[128]{0:T(128)}, f32[128]{0:T(128)S(1)}, u32[]{:S(2)}) copy-start(f32[128]{0:T(128)S(1)} %add_rsqrt_fusion) | copy-start | bytes 1540
  251.6 56.7 %copy-start.3 = (f32[128,2304]{1,0:T(8,128)}, f32[128,2304]{1,0:T(8,128)S(1)}, u32[]{:S(2)}) copy-start(f32[128,2304]{1,0:T(8,128)S(1)} %fusion.81) | copy-start | bytes 3538948
  311.5 316.7 %reduce-scatter.2.cloned.1.call-start = ((), (), s32[]{:S(2)}) async-start(), calls=%async_computation.9 | async-start | bytes 21086208 | tf_op jit(solution)/shard_map/reduce_scatter | solution.py:236
  313.5 16.1 %copy-start.14 = (bf16[128,768]{0,1:T(8,128)(2,1)}, bf16[128,768]{0,1:T(8,128)(2,1)S(1)}, u32[]{:S(2)}) copy-start(bf16[128,768]{0,1:T(8,128)(2,1)S(1)} %copy.28) | copy-start | bytes 589828
  344.8 4.2 copy-start.25
  344.8 4.2 copy-start.29
  372.7 10.3 %copy-start.23 = (f32[128]{0:T(128)S(1)}, f32[128]{0:T(128)}, u32[]{:S(2)}) copy-start(f32[128]{0:T(128)} %copy-done.22) | copy-start | bytes 1540
  372.7 10.3 %copy-start.27 = (f32[128]{0:T(128)S(1)}, f32[128]{0:T(128)}, u32[]{:S(2)}) copy-start(f32[128]{0:T(128)} %copy-done.26) | copy-start | bytes 1540
  (16 other events, 44.7 us)
Sparse Core Ops, SparseCore 0:
  11.0 62.9 all-gather.8
  78.8 25.8 all-gather.10
  106.9 24.0 all-gather.12
  133.9 53.2 all-gather.14
  190.0 58.9 all-gather.16
  251.7 54.3 all-gather.18
  308.2 26.2 all-gather.20
  336.8 24.9 all-gather.22
  413.0 215.2 reduce-scatter.1
where the time goes:
time: 642 us; the launch traced here: 641 us
  waiting for transfers between devices  439 us (68%)
  blocking collectives  72.5 us (11%)
  matrix products  62.9 us (10%)
  local copies, waits for them, and re-layouts  43 us (7%)
  between operations  14.3 us (2%)
  other arithmetic  8.55 us (1%)
    reduce_scatter x1, waiting for transfers between devices, local(): lax.psum_scatter(grad_rows(jnp.int32(0), owned_rows * lax.axis_size(('bat...  210 us
    all_gather x1, waiting for transfers between devices, local(): lax.all_gather(w_inner, ('batch', 'ctx'), axis=0, tiled=True)  59.9 us
    all_gather x1, waiting for transfers between devices, local(): lax.all_gather(w_down, ('batch', 'ctx'), axis=0, tiled=True)  54.4 us
    all_gather x1, waiting for transfers between devices, local(): lax.all_gather(w_proj, ('batch', 'ctx'), axis=0, tiled=True)  49.6 us
    unnamed x1, blocking collectives  42.2 us
    all_gather x1, waiting for transfers between devices, local(): lax.all_gather(key_flat, 'ctx', axis=0, tiled=True)  22.7 us
    concatenate x1, local copies, waits for them, and re-layouts, grad_rows(): jnp.concatenate([jnp.einsum('td,te->de', h_one, d_projected, preferred_el...  22.2 us
    all_gather x1, waiting for transfers between devices, local(): lax.all_gather(value_flat, 'ctx', axis=0, tiled=True)  21.1 us
  transfers between devices with their start and end apart: 9, of which 7 were waited for; matrix products, arithmetic and copies ran while one was open for 8% of the time, Pallas kernels for 0%

commit v1 on v0

--- a/solution.py
+++ b/solution.py
@@ -9,6 +9,18 @@
 FF = 1152
 norm_eps = 1e-05
 rope_base = 160000.0
+
+
+def collect(shard, axis, dim):
+    ways, here = (lax.axis_size(axis), lax.axis_index(axis))
+    grown, reach = (shard, 1)
+    while reach < ways:
+        theirs = lax.ppermute(grown, axis, [(d, d ^ reach) for d in range(ways)])
+        mine_first = jnp.concatenate([grown, theirs], axis=dim)
+        theirs_first = jnp.concatenate([theirs, grown], axis=dim)
+        grown = jnp.where(here & reach == 0, mine_first, theirs_first)
+        reach = 2 * reach
+    return grown
 
 
 def apply_layer_norm(values, gain_vector):
@@ -81,7 +93,7 @@
     score_scale = HEAD_DIM ** (-0.5)
     full_qkv, full_proj, full_inner, full_down, gain_first, gain_second = (
         lax.all_gather(w_qkv, ("batch", "ctx"), axis=0, tiled=True),
-        lax.all_gather(w_proj, ("batch", "ctx"), axis=0, tiled=True),
+        collect(w_proj, ("batch", "ctx"), 0),
         lax.all_gather(w_inner, ("batch", "ctx"), axis=0, tiled=True),
         lax.all_gather(w_down, ("batch", "ctx"), axis=0, tiled=True),
         lax.all_gather(norm1_gain, ("batch", "ctx"), axis=0, tiled=True),

time: 642 us -> 595 us (0.927)
  waiting for transfers between devices: 439 us -> 387 us
    all_gather x1 -> x0, waiting for transfers between devices: 49.6 us -> none  [local(): lax.all_gather(w_proj, ('batch', 'ctx'), axis=0, tiled=True)]
    ppermute x0 -> x5, waiting for transfers between devices: none -> 27.5 us  [collect(): theirs = lax.ppermute(grown, axis, [(d, d ^ reach) for d in range(ways)])]
    all_gather x1, waiting for transfers between devices: 22.7 us -> 0.02 us  [local(): lax.all_gather(key_flat, 'ctx', axis=0, tiled=True)]
  transfers between devices with their start and end apart: 9 -> 13, of which waited for: 7 -> 9; matrix products, arithmetic and copies ran while one was open for 8% -> 9% of each run, Pallas kernels for 0% -> 0%
where the time goes in v1:
time: 595 us; the launch traced here: 594 us
  waiting for transfers between devices  387 us (65%)
  blocking collectives  72.6 us (12%)
  matrix products  61.8 us (10%)
  local copies, waits for them, and re-layouts  43.2 us (7%)
  between operations  14.7 us (2%)
  other arithmetic  8.84 us (1%)
    reduce_scatter x1, waiting for transfers between devices, local(): lax.psum_scatter(grad_rows(jnp.int32(0), owned_rows * lax.axis_size(('bat...  211 us
    all_gather x1, waiting for transfers between devices, local(): lax.all_gather(w_inner, ('batch', 'ctx'), axis=0, tiled=True)  54.7 us
    all_gather x1, waiting for transfers between devices, local(): lax.all_gather(w_down, ('batch', 'ctx'), axis=0, tiled=True)  54.4 us
    unnamed x1, blocking collectives  42.2 us
    ppermute x5, waiting for transfers between devices, collect(): theirs = lax.ppermute(grown, axis, [(d, d ^ reach) for d in range(ways)])  27.5 us
    concatenate x1, local copies, waits for them, and re-layouts, grad_rows(): jnp.concatenate([jnp.einsum('td,te->de', h_one, d_projected, preferred_el...  21.7 us
    all_gather x1, waiting for transfers between devices, local(): lax.all_gather(w_qkv, ('batch', 'ctx'), axis=0, tiled=True)  19.1 us
    all_gather x1, waiting for transfers between devices, local(): lax.all_gather(value_flat, 'ctx', axis=0, tiled=True)  18.6 us
  transfers between devices with their start and end apart: 13, of which 9 were waited for; matrix products, arithmetic and copies ran while one was open for 9% of the time, Pallas kernels for 0%

profile of v1, /device:TPU:0, one launch (start us, length us, event | category | flops | bytes accessed | tf_op | source)
XLA Modules:
  0.0 593.8 jit_solution(10553032929334739325)
XLA Ops:
  9.7 42.2 %all-reduce.2 = (bf16[768]{0:T(1024)(128)(2,1)S(1)}, bf16[768]{0:T(1024)(128)(2,1)S(1)}) all-reduce(bf16[768]{0:T(1024)(128)(2,1)S(1)} %dynamic-update-slice, bf16[768]{0:T(1024)(128)(2,1)S(1)} %dynamic-update-slice.1), channel_id=1, replica_groups=mesh['batch'=4,'ctx'=8] {'batch','ctx'}, use_global_device_ids=true, to_apply=%add | all-reduce | flops 1536 | bytes 6144
  54.8 19.1 %all-gather.8.cloned.1.call-done = bf16[768,2304]{1,0:T(8,128)(2,1)} async-done(((bf16[24,2304]{1,0:T(8,128)(2,1)}), bf16[768,2304]{1,0:T(8,128)(2,1)}) %all-gather.8.cloned.1.call-update) | async-done | bytes 3538960 | tf_op jit(solution)/shard_map/all_gather | solution.py:95
  73.9 2.8 fusion.81
  82.8 3.6 collective-permute-done.1
  87.5 15.8 %collective-permute-done.2 = bf16[96,768]{1,0:T(8,128)(2,1)S(1)} collective-permute-done((bf16[96,768]{1,0:T(8,128)(2,1)S(1)}, bf16[96,768]{1,0:T(8,128)(2,1)S(1)}, u32[]{:S(2)}, u32[]{:S(2)}) %collective-permute-start.2) | collective-permute-done | bytes 147488 | tf_op jit(solution)/shard_map/ppermute | solution.py:18
  104.8 7.2 %collective-permute-done.3 = bf16[192,768]{1,0:T(8,128)(2,1)S(1)} collective-permute-done((bf16[192,768]{1,0:T(8,128)(2,1)S(1)}, bf16[192,768]{1,0:T(8,128)(2,1)S(1)}, u32[]{:S(2)}, u32[]{:S(2)}) %collective-permute-start.3) | collective-permute-done | bytes 294944 | tf_op jit(solution)/shard_map/ppermute | solution.py:18
  114.5 2.5 multiply_reduce_fusion
  119.7 18.6 %all-gather.12.cloned.1.call-done = bf16[1024,768]{1,0:T(8,128)(2,1)} async-done(((bf16[128,768]{1,0:T(8,128)(2,1)}), bf16[1024,768]{1,0:T(8,128)(2,1)}) %all-gather.12.cloned.1.call-update) | async-done | bytes 1572880 | tf_op jit(solution)/shard_map/all_gather | solution.py:123
  140.1 4.8 fusion.35
  145.8 54.7 %all-gather.14.cloned.1.call-done = bf16[768,2304]{1,0:T(8,128)(2,1)} async-done(((bf16[24,2304]{1,0:T(8,128)(2,1)}), bf16[768,2304]{1,0:T(8,128)(2,1)}) %all-gather.14.cloned.1.call-update) | async-done | bytes 3538960 | tf_op jit(solution)/shard_map/all_gather | solution.py:97
  200.4 2.7 fusion.83
  203.1 54.4 %all-gather.16.cloned.1.call-done = bf16[768,1152]{1,0:T(8,128)(2,1)} async-done(((bf16[24,1152]{1,0:T(8,128)(2,1)}), bf16[768,1152]{1,0:T(8,128)(2,1)}) %all-gather.16.cloned.1.call-update) | async-done | bytes 1769488 | tf_op jit(solution)/shard_map/all_gather | solution.py:98
  265.9 15.2 %all_gather.43 = f32[12,1024]{1,0:T(8,128)} all-gather(f32[12,128]{1,0:T(8,128)S(1)} %get-tuple-element.36), channel_id=1, replica_groups=mesh['batch'=4,'ctx'=8] {'ctx'}, dimensions={1}, use_global_device_ids=true | all-gather | bytes 55296 | tf_op jit(solution)/shard_map/all_gather | solution.py:186
  281.2 15.2 %all_gather.45 = f32[12,1024]{1,0:T(8,128)} all-gather(f32[12,128]{1,0:T(8,128)S(1)} %bitcast.126), channel_id=1, replica_groups=mesh['batch'=4,'ctx'=8] {'ctx'}, dimensions={1}, use_global_device_ids=true | all-gather | bytes 55296 | tf_op jit(solution)/shard_map/all_gather | solution.py:187
  300.4 4.1 fusion.59
  304.5 5.1 fusion.87
  309.6 7.3 %fusion.23 = f32[128,12,64]{0,2,1:T(8,128)} fusion(bf16[1024,12,64]{0,2,1:T(8,128)(2,1)} %bitcast.110, f32[12,128,1024]{2,1,0:T(8,128)} %copy-done, f32[12,128]{1,0:T(8,128)S(1)} %bitcast.127, f32[12,128]{1,0:T(8,128)} %copy-done.28, bf16[128,12,64]{0,2,1:T(8,128)(2,1)} %bitcast.118, bf16[1024,12,64]{0,2,1:T(8,128)(2,1)} %bitcast.106), kind=kOutput, calls=%fused_computation.25 | convolution fusion | flops 410615808 | bytes 10039296 | tf_op jit(solution)/shard_map/hqk,khd->qhd/dot_general | solution.py:199
  316.9 2.6 copy.29
  319.5 5.1 fusion.28
  324.6 8.8 %fusion.21 = f32[128,12,64]{0,2,1:T(8,128)} fusion(bf16[1024,12,64]{0,2,1:T(8,128)(2,1)} %bitcast.112, f32[12,1024,128]{2,1,0:T(8,128)} %fusion.87, f32[12,1024]{1,0:T(8,128)} %all_gather.45, f32[12,1024]{1,0:T(8,128)} %all_gather.43, bf16[1024,12,64]{0,2,1:T(8,128)(2,1)} %bitcast.104, bf16[128,12,64]{0,2,1:T(8,128)(2,1)} %bitcast.125), kind=kOutput, calls=%fused_computation.23 | convolution fusion | flops 410615808 | bytes 10125312 | tf_op jit(solution)/shard_map/hqk,qhd->khd/dot_general | solution.py:212
  335.0 5.3 fusion.61
  340.2 2.6 fusion.57
  343.7 21.7 %concatenate.71 = f32[768,6530]{1,0:T(8,128)} concatenate(f32[768,2304]{1,0:T(8,128)} %fusion.61, f32[768,768]{1,0:T(8,128)} %fusion.66, f32[768,2304]{1,0:T(8,128)} %fusion.59, f32[768,1152]{1,0:T(8,128)S(1)} %convolution_bitcast_fusion, f32[768,1]{1,0:T(8,128)} %broadcast_in_dim.18, f32[768,1]{1,0:T(8,128)} %broadcast_in_dim.19), dimensions={1} | concatenate | bytes 40120320 | tf_op jit(solution)/shard_map/concatenate | solution.py:235
  369.7 210.9 %reduce-scatter.2.cloned.1.call-done = f32[24,6530]{1,0:T(8,128)} async-done(((f32[768,6530]{1,0:T(8,128)}), f32[24,6530]{1,0:T(8,128)}) %reduce-scatter.2.cloned.1.call-update) | async-done | bytes 626896 | tf_op jit(solution)/shard_map/reduce_scatter | solution.py:248
  (157 shorter events, 46.8 us)
Async XLA Ops:
  7.2 66.8 %all-gather.8.cloned.1.call-start = ((), (), s32[]{:S(2)}) async-start(), calls=%async_computation.1 | async-start | bytes 3649536 | tf_op jit(solution)/shard_map/all_gather | solution.py:95
  7.9 106.6 %all-gather.10.cloned.1.call-start = ((), (), s32[]{:S(2)}) async-start(), calls=%async_computation.2 | async-start | bytes 1769472 | tf_op jit(solution)/shard_map/all_gather | solution.py:122
  52.9 23.8 %copy-start.29 = (f32[128]{0:T(128)}, f32[128]{0:T(128)S(1)}, u32[]{:S(2)}) copy-start(f32[128]{0:T(128)S(1)} %broadcast_multiply_fusion.6) | copy-start | bytes 1540
  54.1 22.7 %copy-start.33 = (f32[128]{0:T(128)}, f32[128]{0:T(128)S(1)}, u32[]{:S(2)}) copy-start(f32[128]{0:T(128)S(1)} %add_rsqrt_fusion.1) | copy-start | bytes 1540
  54.8 22.3 %copy-start.26 = (f32[128,32]{0,1:T(8,128)}, f32[128,32]{0,1:T(8,128)S(1)}, u32[]{:S(2)}) copy-start(f32[128,32]{0,1:T(8,128)S(1)} %get-tuple-element.40) | copy-start | bytes 49156
  78.7 59.7 %all-gather.12.cloned.1.call-start = ((), (), s32[]{:S(2)}) async-start(), calls=%async_computation.3 | async-start | bytes 1769472 | tf_op jit(solution)/shard_map/all_gather | solution.py:123
  79.4 121.0 %all-gather.14.cloned.1.call-start = ((), (), s32[]{:S(2)}) async-start(), calls=%async_computation.4 | async-start | bytes 3649536 | tf_op jit(solution)/shard_map/all_gather | solution.py:97
  80.0 177.5 %all-gather.16.cloned.1.call-start = ((), (), s32[]{:S(2)}) async-start(), calls=%async_computation.5 | async-start | bytes 1824768 | tf_op jit(solution)/shard_map/all_gather | solution.py:98
  80.6 223.9 %all-gather.18.cloned.1.call-start = ((), (), s32[]{:S(2)}) async-start(), calls=%async_computation.6 | async-start | bytes 1769472 | tf_op jit(solution)/shard_map/all_gather | solution.py:203
  80.7 1.3 collective-permute-start
  82.0 4.5 collective-permute-start.1
  86.5 16.8 %collective-permute-start.2 = (bf16[96,768]{1,0:T(8,128)(2,1)S(1)}, bf16[96,768]{1,0:T(8,128)(2,1)S(1)}, u32[]{:S(2)}, u32[]{:S(2)}) collective-permute-start(bf16[96,768]{1,0:T(8,128)(2,1)S(1)} %maximum_select_fusion.5), channel_id=1, source_target_pairs={{0,4},{1,5},{2,6},{3,7},{4,0},{5,1},{6,2},{7,3},{8,12},{9,13},{10,... | collective-permute-start | bytes 442376 | tf_op jit(solution)/shard_map/ppermute | solution.py:18
  103.3 8.7 %collective-permute-start.3 = (bf16[192,768]{1,0:T(8,128)(2,1)S(1)}, bf16[192,768]{1,0:T(8,128)(2,1)S(1)}, u32[]{:S(2)}, u32[]{:S(2)}) collective-permute-start(bf16[192,768]{1,0:T(8,128)(2,1)S(1)} %maximum_select_fusion.2), channel_id=1, source_target_pairs={{0,8},{1,9},{2,10},{3,11},{4,12},{5,13},{6,14},{7,15},{8,0},{9,1},... | collective-permute-start | bytes 884744 | tf_op jit(solution)/shard_map/ppermute | solution.py:18
  112.2 32.7 %collective-permute-start.4 = (bf16[384,768]{1,0:T(8,128)(2,1)S(1)}, bf16[384,768]{1,0:T(8,128)(2,1)S(1)}, u32[]{:S(2)}, u32[]{:S(2)}) collective-permute-start(bf16[384,768]{1,0:T(8,128)(2,1)S(1)} %maximum_select_fusion.1), channel_id=1, source_target_pairs={{0,16},{1,17},{2,18},{3,19},{4,20},{5,21},{6,22},{7,23},{8,24},{9,... | collective-permute-start | bytes 1769480 | tf_op jit(solution)/shard_map/ppermute | solution.py:18
  114.5 202.5 %all-gather.20.cloned.1.call-start = ((), (), s32[]{:S(2)}) async-start(), calls=%async_computation.7 | async-start | bytes 1769472 | tf_op jit(solution)/shard_map/all_gather | solution.py:204
  119.7 146.2 %copy-start.28 = (f32[12,128]{1,0:T(8,128)}, f32[12,128]{1,0:T(8,128)S(1)}, u32[]{:S(2)}) copy-start(f32[12,128]{1,0:T(8,128)S(1)} %get-tuple-element.36) | copy-start | bytes 18436
  145.5 116.0 %copy-start.1 = (f32[128,768]{1,0:T(8,128)}, f32[128,768]{1,0:T(8,128)S(1)}, u32[]{:S(2)}) copy-start(f32[128,768]{1,0:T(8,128)S(1)} %get-tuple-element.44) | copy-start | bytes 1179652
  145.5 116.0 %copy-start.31 = (f32[128]{0:T(128)}, f32[128]{0:T(128)S(1)}, u32[]{:S(2)}) copy-start(f32[128]{0:T(128)S(1)} %broadcast_multiply_fusion.5) | copy-start | bytes 1540
  145.7 115.8 %copy-start.35 = (f32[128]{0:T(128)}, f32[128]{0:T(128)S(1)}, u32[]{:S(2)}) copy-start(f32[128]{0:T(128)S(1)} %add_rsqrt_fusion) | copy-start | bytes 1540
  145.8 111.8 %copy-start.18 = (bf16[1,128,768]{2,1,0:T(8,128)(2,1)S(1)}, bf16[1,128,768]{2,1,0:T(8,128)(2,1)}, u32[]{:S(2)}) copy-start(bf16[1,128,768]{2,1,0:T(8,128)(2,1)} %param.9) | copy-start | bytes 589828
  203.1 58.4 %copy-start.7 = (f32[128,2304]{1,0:T(8,128)}, f32[128,2304]{1,0:T(8,128)S(1)}, u32[]{:S(2)}) copy-start(f32[128,2304]{1,0:T(8,128)S(1)} %fusion.83) | copy-start | bytes 3538948
  261.8 34.6 %copy-start.11 = (f32[128,768]{1,0:T(8,128)}, f32[128,768]{1,0:T(8,128)S(1)}, u32[]{:S(2)}) copy-start(f32[128,768]{1,0:T(8,128)S(1)} %multiply_add_fusion) | copy-start | bytes 1179652
  263.1 317.6 %reduce-scatter.2.cloned.1.call-start = ((), (), s32[]{:S(2)}) async-start(), calls=%async_computation.8 | async-start | bytes 21086208 | tf_op jit(solution)/shard_map/reduce_scatter | solution.py:248
  265.0 31.4 %copy-start.19 = (bf16[128,768]{0,1:T(8,128)(2,1)}, bf16[128,768]{0,1:T(8,128)(2,1)S(1)}, u32[]{:S(2)}) copy-start(bf16[128,768]{0,1:T(8,128)(2,1)S(1)} %copy.28) | copy-start | bytes 589828
  (27 other events, 82.0 us)
Sparse Core Ops, SparseCore 0:
  11.0 62.9 all-gather.7
  78.8 31.5 all-gather.9
  112.6 25.7 all-gather.11
  141.2 59.1 all-gather.13
  203.1 54.3 all-gather.15
  259.6 26.2 all-gather.17
  288.1 24.1 all-gather.19
  365.6 215.0 reduce-scatter.1
